TPU v7x, 256 devices: a whole 4x4x8 slice. The times are simulated.
256 devices in a mesh: row: 16 (over y, x), col: 16 (over z, core).
Axes of the slice: x: 4, y: 4, z: 8, core: 2. Of those that a mesh axis runs over, the one named last changes fastest.
Arguments:
- factor_diag: float32 [2, 512, 512], replicated, as said below
- factor_mid: float32 [512, 512], replicated, may hold values from -0.25 to 0.25
- factor_low: float32 [2, 16384, 512], P(None, ('row', 'col')), may hold values from -0.046875 to 0.046875
- adjoint_diag: float32 [2, 512, 512], replicated, may hold values from -6 to 6
- adjoint_mid: float32 [512, 512], replicated, may hold values from -6 to 6
- adjoint_low: float32 [2, 16384, 512], P(None, ('row', 'col')), may hold values from -6 to 6
- trailing_adjoint: float32 [16384, 16, 1024], P('row', None, 'col'), as said below
Outputs:
- grad_diag: float32 [2, 512, 512], replicated
- grad_mid: float32 [512, 512], replicated
- grad_low: float32 [2, 16384, 512], P(None, ('row', 'col'))
Inputs may be any that keep to these rules, and one draw needn't show every extreme that they name: `factor_diag`: each of the two [512, 512] blocks is lower triangular with diagonal entries between 1 and 2. `trailing_adjoint`: symmetric when read as an 16384 x 16384 matrix in row-major order.
All inputs are finite; a program needn't handle non-finite values.
Results may differ from a plain program's by a relative error of at most 0.000065.
Values sent between devices are 32-bit elements; how exact they have to be, the bound alone decides.
No kernel may reach another device: no remote copies, remote signals or barrier semaphores. Data moves between devices by JAX's collectives and lax.ppermute only.
A program may use at most 128 MiB of HBM per device.

v0:
```python
import jax
import jax.numpy as jnp
from jax import lax
from jax.sharding import PartitionSpec as P


def lower_half(matrix):
    return jnp.tril(matrix, -1) + 0.5 * jnp.diag(jnp.diag(matrix))


def product(left_side, right_side):
    return jnp.dot(
        left_side, right_side, precision=lax.Precision.HIGHEST, preferred_element_type=jnp.float32
    )


def right_solve(factor, row_block):
    return jax.scipy.linalg.solve_triangular(factor, row_block.T, trans=1, lower=True).T


def diag_adjoint(factor, adjoint):
    inner_term = lower_half(product(factor.T, adjoint))
    halfway = jax.scipy.linalg.solve_triangular(factor, inner_term, trans=1, lower=True)
    whole_term = right_solve(factor, halfway)
    return 0.5 * (whole_term + whole_term.T)


def shards(
    factor_diag, factor_mid, factor_low, adjoint_diag, adjoint_mid, adjoint_low, trailing_adjoint
):
    block_rows, row_groups, group_cols = trailing_adjoint.shape
    local_block = trailing_adjoint.reshape(block_rows, row_groups * group_cols)

    def image_of(panel):
        columns = lax.all_gather(panel, "row", axis=0, tiled=True)
        return lax.psum_scatter(
            product(local_block, columns), "col", scatter_dimension=0, tiled=True
        )

    second_image = image_of(factor_low[1])
    first_image = image_of(factor_low[0])
    second_solved = right_solve(factor_diag[1], adjoint_low[1] - 2.0 * second_image)
    second_total = lax.psum(product(second_solved.T, factor_low[1]), ("row", "col"))
    second_grad = diag_adjoint(factor_diag[1], adjoint_diag[1] - second_total)
    second_half = 0.5 * second_solved
    upper_term = product(second_half.T, factor_low[0])
    bottom_rows = adjoint_low[0] - 2.0 * (product(second_half, factor_mid) + first_image)
    bottom_solved = right_solve(factor_diag[0], bottom_rows)
    lower_term = product(bottom_solved.T, factor_low[0])
    upper_total = lax.psum(upper_term, ("row", "col"))
    lower_total = lax.psum(lower_term, ("row", "col"))
    top_rows = adjoint_mid - 2.0 * (product(second_grad, factor_mid) + upper_total)
    top_solved = right_solve(factor_diag[0], top_rows)
    first_adjoint = adjoint_diag[0] - product(top_solved.T, factor_mid) - lower_total
    first_grad = diag_adjoint(factor_diag[0], first_adjoint)
    return (
        jnp.stack([first_grad, second_grad]),
        0.5 * top_solved,
        jnp.stack([0.5 * bottom_solved, second_half]),
    )


def solution(mesh):
    return jax.shard_map(
        shards,
        mesh=mesh,
        in_specs=(
            P(),
            P(),
            P(None, ("row", "col"), None),
            P(),
            P(),
            P(None, ("row", "col"), None),
            P("row", None, "col"),
        ),
        out_specs=(P(), P(), P(None, ("row", "col"), None)),
        check_vma=False,
    )
```

profile of v0, /device:TPU:2, one launch (start us, length us, event | category | flops | bytes accessed | tf_op | source)
XLA Modules:
  0.0 587.7 jit_solution(3043104510383694873)
XLA Ops:
  7.2 1.8 fusion.165
  9.8 53.8 %all-gather.5.cloned.1.call-done = f32[1,1024,512]{2,1,0:T(8,128)} async-done(((f32[1,64,512]{2,1,0:T(8,128)}), f32[1,1024,512]{2,1,0:T(8,128)}) %all-gather.5.cloned.1.call-update) | async-done | bytes 2097168 | tf_op jit(solution)/shard_map/all_gather | solution.py:35
  63.6 10.2 %fusion.2 = f32[1024,512]{1,0:T(8,128)} fusion(f32[1024,1024]{0,1:T(8,128)} %bitcast.202, f32[1,1024,512]{2,1,0:T(8,128)} %all-gather.5.cloned.1.call-done), kind=kOutput, calls=%fused_computation.9 | convolution fusion | flops 6442450944 | bytes 8388608 | tf_op jit(solution)/shard_map/dot_general | solution.py:12
  73.8 1.5 copy-done.1
  75.3 1.6 bitcast_select_fusion.1
  76.9 39.0 %all-gather.7.cloned.1.call-done = f32[1,1024,512]{2,1,0:T(8,128)} async-done(((f32[1,64,512]{2,1,0:T(8,128)}), f32[1,1024,512]{2,1,0:T(8,128)}) %all-gather.7.cloned.1.call-update) | async-done | bytes 2097168 | tf_op jit(solution)/shard_map/all_gather | solution.py:35
  115.9 10.2 %fusion = f32[1024,512]{1,0:T(8,128)} fusion(f32[1024,1024]{0,1:T(8,128)} %bitcast.203, f32[1,1024,512]{2,1,0:T(8,128)} %all-gather.7.cloned.1.call-done), kind=kOutput, calls=%fused_computation.7 | convolution fusion | flops 6442450944 | bytes 8388608 | tf_op jit(solution)/shard_map/dot_general | solution.py:12
  126.4 12.0 %while.14 = (s32[]{:T(128)}, f32[512,512]{1,0:T(8,128)}, s32[4,2]{0,1:T(2,128)S(1)}, f32[4,128,128]{2,1,0:T(8,128)S(1)}, s32[]{:T(128)}) while((s32[]{:T(128)}, f32[512,512]{1,0:T(8,128)}, s32[4,2]{0,1:T(2,128)S(1)}, f32[4,128,128]{2,1,0:T(8,128)S(1)}, s32[]{:T(128)}) %tuple.62), condition=%wide.while_cond.1.clone, body=%wide.while_body.1.clone.sunk | while | flops 2 | bytes 131181 | solution.py:18
  127.1 2.3 bitcast_dynamic-update-slice_fusion.4
  130.1 2.3 bitcast_dynamic-update-slice_fusion.4
  133.1 2.3 bitcast_dynamic-update-slice_fusion.4
  136.2 2.3 bitcast_dynamic-update-slice_fusion.4
  138.5 39.3 %custom-call.17 = f32[4,128,128]{1,2,0:T(8,128)S(1)} custom-call(f32[4,128,128]{2,1,0:T(8,128)S(1)} %get-tuple-element.53), custom_call_target="InvertDiagBlocksLowerTriangular" | custom-call | tf_op jit(solution)/shard_map/jit(_solve_triangular)/triangular_solve | solution.py:18
  177.8 7.7 %while.15 = (s32[]{:T(128)}, f32[512,512]{1,0:T(8,128)S(1)}, s32[4,2]{0,1:T(2,128)S(1)}, f32[4,128,128]{2,1,0:T(8,128)S(1)}, s32[]{:T(128)}) while((s32[]{:T(128)}, f32[512,512]{1,0:T(8,128)S(1)}, s32[4,2]{0,1:T(2,128)S(1)}, f32[4,128,128]{2,1,0:T(8,128)S(1)}, s32[]{:T(128)}) %tuple.80), condition=%wide.while_cond.1.clone.3, body=%wide.while_body.1.clone.3.sunk | while | flops 2 | bytes 131181 | solution.py:18
  186.2 40.1 %custom-call.21 = f32[4,128,128]{1,2,0:T(8,128)S(1)} custom-call(f32[4,128,128]{2,1,0:T(8,128)} %copy-done.21), custom_call_target="InvertDiagBlocksLowerTriangular" | custom-call | tf_op jit(solution)/shard_map/jit(_solve_triangular)/triangular_solve | solution.py:18
  231.7 2.0 fusion.77
  233.8 2.0 fusion.79
  235.8 5.0 reduce-scatter.5.cloned.1.call-done
  240.7 1.7 fusion.10
  244.1 2.0 fusion.75
  247.0 265.8 %all-reduce.3.cloned.1.call-done = (f32[512,512]{1,0:T(8,128)}, f32[512,512]{1,0:T(8,128)}, f32[512,512]{1,0:T(8,128)}) async-done(((f32[512,512]{1,0:T(8,128)}, f32[512,512]{1,0:T(8,128)}, f32[512,512]{1,0:T(8,128)}), (f32[512,512]{1,0:T(8,128)}, f32[512,512]{1,0:T(8,128)}, f32[512,512]{1,0:T(8,128)})) %all-reduce.3.cloned.1.call-update) | async-done | bytes 3145744 | tf_op jit(solution)/shard_map/psum | solution.py:43
  512.8 3.7 convolution_bitcast_fusion.1
  516.5 4.8 gather_fusion
  534.6 1.6 copy.29
  536.2 3.8 fusion.7
  543.9 2.2 convolution_subtract_fusion.13
  548.4 1.5 fusion.123
  550.9 3.4 fusion.4
  554.3 1.9 convolution_bitcast_fusion
  556.2 4.7 gather_fusion.1
  576.9 2.1 multiply_bitcast_fusion.1
  579.2 1.8 copy.39
  (148 shorter events, 56.0 us)
Async XLA Ops:
  7.2 233.6 %copy-start = (f32[512,512]{1,0:T(8,128)S(1)}, f32[512,512]{1,0:T(8,128)}, u32[]{:S(2)}) copy-start(f32[512,512]{1,0:T(8,128)} %param.12) | copy-start | bytes 3145732
  7.2 56.4 %all-gather.5.cloned.1.call-start = ((), (), s32[]{:S(2)}) async-start(), calls=%async_computation.4 | async-start | bytes 2228224 | tf_op jit(solution)/shard_map/all_gather | solution.py:35
  9.0 106.9 %all-gather.7.cloned.1.call-start = ((), (), s32[]{:S(2)}) async-start(), calls=%async_computation.5 | async-start | bytes 2228224 | tf_op jit(solution)/shard_map/all_gather | solution.py:35
  9.8 216.6 %reduce-scatter.3.cloned.1.call-start = ((), (), s32[]{:S(2)}) async-start(), calls=%async_computation.2 | async-start | bytes 2228224 | tf_op jit(solution)/shard_map/reduce_scatter | solution.py:36
  73.8 1.6 copy-start.1
  73.8 166.9 %reduce-scatter.5.cloned.1.call-start = ((), (), s32[]{:S(2)}) async-start(), calls=%async_computation.3 | async-start | bytes 2228224 | tf_op jit(solution)/shard_map/reduce_scatter | solution.py:36
  126.1 51.7 %copy-start.3 = (f32[512,512]{1,0:T(8,128)S(1)}, f32[512,512]{1,0:T(8,128)}, u32[]{:S(2)}) copy-start(f32[512,512]{1,0:T(8,128)} %get-tuple-element.169) | copy-start | bytes 3145732
  126.1 100.3 %copy-start.20 = (f32[2,64,512]{2,1,0:T(8,128)S(1)}, f32[2,64,512]{2,1,0:T(8,128)}, u32[]{:S(2)}) copy-start(f32[2,64,512]{2,1,0:T(8,128)} %param.16) | copy-start | bytes 786436
  126.1 105.6 %copy-start.19 = (f32[2,64,512]{2,1,0:T(8,128)S(1)}, f32[2,64,512]{2,1,0:T(8,128)}, u32[]{:S(2)}) copy-start(f32[2,64,512]{2,1,0:T(8,128)} %param.13) | copy-start | bytes 786436
  126.2 386.6 %all-reduce.3.cloned.1.call-start = ((), (), s32[]{:S(2)}) async-start(), calls=%async_computation.6 | async-start | bytes 6291456 | tf_op jit(solution)/shard_map/psum | solution.py:43
  177.8 351.5 %copy-start.15 = (f32[4,128,128]{1,2,0:T(8,128)}, f32[4,128,128]{1,2,0:T(8,128)S(1)}, u32[]{:S(2)}) copy-start(f32[4,128,128]{1,2,0:T(8,128)S(1)} %custom-call.17) | copy-start | bytes 786436
  185.5 0.7 copy-start.21
  226.3 19.8 %copy-start.6 = (f32[4,128,128]{1,2,0:T(8,128)}, f32[4,128,128]{1,2,0:T(8,128)S(1)}, u32[]{:S(2)}) copy-start(f32[4,128,128]{1,2,0:T(8,128)S(1)} %custom-call.21) | copy-start | bytes 786436
  521.3 1.2 copy-start.5
  531.2 4.9 copy-start.9
  531.4 1.4 copy-start.11
  531.5 1.3 copy-start.12
  532.8 0.7 copy-start.13
  536.2 3.8 copy-start.7
  541.8 1.4 copy-start.14
  543.2 0.7 copy-start.16
  548.4 2.6 copy-start.18
  550.9 3.4 copy-start.2
  556.2 4.9 copy-start.8
  561.0 1.2 copy-start.4
  573.7 0.7 copy-start.17
  574.4 2.5 copy-start.10
Sparse Core Ops, SparseCore 0:
  11.0 52.5 all-gather.4
  66.6 49.3 all-gather.6
  119.0 60.2 reduce-scatter.2
  181.7 58.9 reduce-scatter.4
  246.9 265.8 all-reduce.2
where the time goes:
time: 594 us; the launch traced here: 588 us
  waiting for transfers between devices  364 us (61%)
  other arithmetic  88.8 us (15%)
  matrix products  72.9 us (12%)
  local copies, waits for them, and re-layouts  46.4 us (8%)
  between operations  14.8 us (2%)
    psum x1, waiting for transfers between devices, shards(): lax.psum(product(second_solved.T, factor_low[1]), ('row', 'col'))  266 us
    all_gather x2, waiting for transfers between devices, image_of(): columns = lax.all_gather(panel, 'row', axis=0, tiled=True)  92.8 us
    another operation x4, other arithmetic, right_solve(): jax.scipy.linalg.solve_triangular(factor, row_block.T, trans=1, lower=True)  81 us
    dot_general x10, matrix products, product(): jnp.dot(left_side, right_side, precision=lax.Precision.HIGHEST, preferred...  41 us
    another operation x36, local copies, waits for them, and re-layouts, right_solve(): jax.scipy.linalg.solve_triangular(factor, row_block.T, trans=1, lower=True)  24.7 us
    another operation x35, matrix products, right_solve(): jax.scipy.linalg.solve_triangular(factor, row_block.T, trans=1, lower=True)  22.8 us
  transfers between devices with their start and end apart: 5, of which 4 were waited for; matrix products, arithmetic and copies ran while one was open for 22% of the time, Pallas kernels for 0%

commit v1 on v0

--- a/solution.py
+++ b/solution.py
@@ -2,6 +2,13 @@
 import jax.numpy as jnp
 from jax import lax
 from jax.sharding import PartitionSpec as P
+
+
+def swapped_in(array, name, along):
+    n_dev = lax.axis_size(name)
+    blocks = jnp.stack([array for _ in range(n_dev)])
+    blocks = lax.all_to_all(blocks, name, split_axis=0, concat_axis=0)
+    return jnp.concatenate(blocks, axis=along)
 
 
 def lower_half(matrix):
@@ -32,7 +39,7 @@
     local_block = trailing_adjoint.reshape(block_rows, row_groups * group_cols)
 
     def image_of(panel):
-        columns = lax.all_gather(panel, "row", axis=0, tiled=True)
+        columns = swapped_in(panel, "row", 0)
         return lax.psum_scatter(
             product(local_block, columns), "col", scatter_dimension=0, tiled=True
         )

time: 594 us -> 564 us (0.949)
  waiting for transfers between devices: 364 us -> 293 us
  blocking collectives: 0 us -> 34.6 us
    all_gather x2 -> x0, waiting for transfers between devices: 92.8 us -> none  [image_of(): columns = lax.all_gather(panel, 'row', axis=0, tiled=True)]
    all_to_all x0 -> x1, blocking collectives: none -> 34.6 us  [swapped_in(): blocks = lax.all_to_all(blocks, name, split_axis=0, concat_axis=0)]
    all_to_all x0 -> x1, waiting for transfers between devices: none -> 24.6 us  [swapped_in(): blocks = lax.all_to_all(blocks, name, split_axis=0, concat_axis=0)]
  transfers between devices with their start and end apart: 5 -> 4, of which waited for: 4 -> 2; matrix products, arithmetic and copies ran while one was open for 22% -> 22% of each run, Pallas kernels for 0% -> 0%
where the time goes in v1:
time: 564 us; the launch traced here: 555 us
  waiting for transfers between devices  293 us (52%)
  other arithmetic  88.8 us (16%)
  matrix products  70.8 us (13%)
  local copies, waits for them, and re-layouts  46.5 us (8%)
  blocking collectives  34.6 us (6%)
  between operations  14.8 us (3%)
  starting transfers between devices  6.04 us (1%)
    psum x1, waiting for transfers between devices, shards(): lax.psum(product(second_solved.T, factor_low[1]), ('row', 'col'))  268 us
    another operation x4, other arithmetic, right_solve(): jax.scipy.linalg.solve_triangular(factor, row_block.T, trans=1, lower=True)  81 us
    dot_general x10, matrix products, product(): jnp.dot(left_side, right_side, precision=lax.Precision.HIGHEST, preferred...  38.9 us
    all_to_all x1, blocking collectives, swapped_in(): blocks = lax.all_to_all(blocks, name, split_axis=0, concat_axis=0)  34.6 us
    another operation x36, local copies, waits for them, and re-layouts, right_solve(): jax.scipy.linalg.solve_triangular(factor, row_block.T, trans=1, lower=True)  25.2 us
    all_to_all x1, waiting for transfers between devices, swapped_in(): blocks = lax.all_to_all(blocks, name, split_axis=0, concat_axis=0)  24.6 us
    another operation x35, matrix products, right_solve(): jax.scipy.linalg.solve_triangular(factor, row_block.T, trans=1, lower=True)  22.8 us
  transfers between devices with their start and end apart: 4, of which 2 were waited for; matrix products, arithmetic and copies ran while one was open for 22% of the time, Pallas kernels for 0%

profile of v1, /device:TPU:2, one launch (start us, length us, event | category | flops | bytes accessed | tf_op | source)
XLA Modules:
  0.0 554.6 jit_solution(13381320104166079622)
XLA Ops:
  8.6 34.6 %all_to_all.10 = f32[16,64,512]{2,1,0:T(8,128)S(1)} all-to-all(f32[16,64,512]{2,1,0:T(8,128)S(1)} %stack.24), channel_id=1, replica_groups=mesh['row'=16,'col'=16] {'row'}, dimensions={0} | all-to-all | bytes 4194304 | tf_op jit(solution)/shard_map/all_to_all | solution.py:10
  43.1 8.1 %convolution_bitcast_fusion.1 = f32[1024,512]{1,0:T(8,128)} fusion(f32[1024,16,64]{0,2,1:T(8,128)S(1)} %copy-done.22, f32[16,64,512]{2,1,0:T(8,128)S(1)} %all_to_all.10), kind=kOutput, calls=%fused_computation.8 | convolution fusion | flops 6442450944 | bytes 8388608 | tf_op jit(solution)/shard_map/dot_general | solution.py:19
  51.2 1.6 stack.25
  52.8 5.7 %all-to-all-start.1 = ((f32[16,64,512]{2,1,0:T(8,128)}), f32[16,64,512]{2,1,0:T(8,128)}, u32[]{:S(2)}, u32[]{:S(2)}) async-start(f32[16,64,512]{2,1,0:T(8,128)} %stack.25), calls=%async_computation.2 | async-start | bytes 4194304 | tf_op jit(solution)/shard_map/all_to_all | solution.py:10
  58.7 1.6 bitcast_select_fusion.1
  60.2 24.6 %all-to-all-done.1 = f32[16,64,512]{2,1,0:T(8,128)} async-done(((f32[16,64,512]{2,1,0:T(8,128)}), f32[16,64,512]{2,1,0:T(8,128)}, u32[]{:S(2)}, u32[]{:S(2)}) %all-to-all-start.1) | async-done | bytes 2097184 | tf_op jit(solution)/shard_map/all_to_all | solution.py:10
  84.8 10.2 %convolution_bitcast_fusion = f32[1024,512]{1,0:T(8,128)} fusion(f32[1024,16,64]{0,2,1:T(8,128)} %param.17, f32[16,64,512]{2,1,0:T(8,128)} %all-to-all-done.1), kind=kOutput, calls=%fused_computation.7 | convolution fusion | flops 6442450944 | bytes 8388608 | tf_op jit(solution)/shard_map/dot_general | solution.py:19
  95.3 12.2 %while.14 = (s32[]{:T(128)}, f32[512,512]{1,0:T(8,128)}, s32[4,2]{0,1:T(2,128)S(1)}, f32[4,128,128]{2,1,0:T(8,128)S(1)}, s32[]{:T(128)}) while((s32[]{:T(128)}, f32[512,512]{1,0:T(8,128)}, s32[4,2]{0,1:T(2,128)S(1)}, f32[4,128,128]{2,1,0:T(8,128)S(1)}, s32[]{:T(128)}) %tuple.62), condition=%wide.while_cond.1.clone, body=%wide.while_body.1.clone.sunk | while | flops 2 | bytes 131181 | solution.py:25
  96.0 2.4 bitcast_dynamic-update-slice_fusion.4
  99.0 2.4 bitcast_dynamic-update-slice_fusion.4
  102.1 2.4 bitcast_dynamic-update-slice_fusion.4
  105.2 2.3 bitcast_dynamic-update-slice_fusion.4
  107.5 39.3 %custom-call.17 = f32[4,128,128]{1,2,0:T(8,128)S(1)} custom-call(f32[4,128,128]{2,1,0:T(8,128)S(1)} %get-tuple-element.53), custom_call_target="InvertDiagBlocksLowerTriangular" | custom-call | tf_op jit(solution)/shard_map/jit(_solve_triangular)/triangular_solve | solution.py:25
  146.9 7.9 %while.15 = (s32[]{:T(128)}, f32[512,512]{1,0:T(8,128)S(1)}, s32[4,2]{0,1:T(2,128)S(1)}, f32[4,128,128]{2,1,0:T(8,128)S(1)}, s32[]{:T(128)}) while((s32[]{:T(128)}, f32[512,512]{1,0:T(8,128)S(1)}, s32[4,2]{0,1:T(2,128)S(1)}, f32[4,128,128]{2,1,0:T(8,128)S(1)}, s32[]{:T(128)}) %tuple.76), condition=%wide.while_cond.1.clone.3, body=%wide.while_body.1.clone.3.sunk | while | flops 2 | bytes 131181 | solution.py:25
  155.6 40.1 %custom-call.21 = f32[4,128,128]{1,2,0:T(8,128)S(1)} custom-call(f32[4,128,128]{2,1,0:T(8,128)} %copy-done.21), custom_call_target="InvertDiagBlocksLowerTriangular" | custom-call | tf_op jit(solution)/shard_map/jit(_solve_triangular)/triangular_solve | solution.py:25
  201.1 2.0 fusion.76
  203.1 2.0 fusion.151
  205.1 1.7 fusion.6
  208.5 2.0 fusion.92
  211.4 268.3 %all-reduce.3.cloned.1.call-done = (f32[512,512]{1,0:T(8,128)}, f32[512,512]{1,0:T(8,128)}, f32[512,512]{1,0:T(8,128)}) async-done(((f32[512,512]{1,0:T(8,128)}, f32[512,512]{1,0:T(8,128)}, f32[512,512]{1,0:T(8,128)}), (f32[512,512]{1,0:T(8,128)}, f32[512,512]{1,0:T(8,128)}, f32[512,512]{1,0:T(8,128)})) %all-reduce.3.cloned.1.call-update) | async-done | bytes 3145744 | tf_op jit(solution)/shard_map/psum | solution.py:50
  479.7 3.7 convolution_bitcast_fusion.3
  483.4 4.8 gather_fusion
  501.5 1.6 copy.29
  503.0 3.8 fusion.3
  510.8 2.2 convolution_subtract_fusion.13
  515.3 1.5 fusion.115
  517.8 3.4 fusion
  521.2 1.9 convolution_bitcast_fusion.2
  523.1 4.7 gather_fusion.1
  531.4 1.5 convolution_subtract_fusion.12
  543.8 2.1 multiply_bitcast_fusion.1
  546.1 1.8 copy.39
  (149 shorter events, 55.3 us)
Async XLA Ops:
  7.2 198.0 %copy-start = (f32[512,512]{1,0:T(8,128)S(1)}, f32[512,512]{1,0:T(8,128)}, u32[]{:S(2)}) copy-start(f32[512,512]{1,0:T(8,128)} %param.12) | copy-start | bytes 3145732
  7.2 188.5 %reduce-scatter.3.cloned.1.call-start = ((), (), s32[]{:S(2)}) async-start(), calls=%async_computation.4 | async-start | bytes 2228224 | tf_op jit(solution)/shard_map/reduce_scatter | solution.py:43
  8.6 34.6 %copy-start.22 = (f32[1024,16,64]{0,2,1:T(8,128)S(1)}, f32[1024,16,64]{0,2,1:T(8,128)}, u32[]{:S(2)}) copy-start(f32[1024,16,64]{0,2,1:T(8,128)} %param.17) | copy-start | bytes 12582916
  52.8 5.8 %copy-start.1 = (f32[2,512,512]{2,1,0:T(8,128)S(1)}, f32[2,512,512]{2,1,0:T(8,128)}, u32[]{:S(2)}) copy-start(f32[2,512,512]{2,1,0:T(8,128)} %param.11) | copy-start | bytes 6291460
  52.8 32.0 %all-to-all-start.1 = ((f32[16,64,512]{2,1,0:T(8,128)}), f32[16,64,512]{2,1,0:T(8,128)}, u32[]{:S(2)}, u32[]{:S(2)}) async-start(f32[16,64,512]{2,1,0:T(8,128)} %stack.25), calls=%async_computation.2 | async-start | bytes 4194304 | tf_op jit(solution)/shard_map/all_to_all | solution.py:10
  58.6 146.5 %reduce-scatter.5.cloned.1.call-start = ((), (), s32[]{:S(2)}) async-start(), calls=%async_computation.5 | async-start | bytes 2228224 | tf_op jit(solution)/shard_map/reduce_scatter | solution.py:43
  95.0 51.9 %copy-start.3 = (f32[512,512]{1,0:T(8,128)S(1)}, f32[512,512]{1,0:T(8,128)}, u32[]{:S(2)}) copy-start(f32[512,512]{1,0:T(8,128)} %get-tuple-element.169) | copy-start | bytes 3145732
  95.0 100.7 %copy-start.20 = (f32[2,64,512]{2,1,0:T(8,128)S(1)}, f32[2,64,512]{2,1,0:T(8,128)}, u32[]{:S(2)}) copy-start(f32[2,64,512]{2,1,0:T(8,128)} %param.16) | copy-start | bytes 786436
  95.0 106.1 %copy-start.19 = (f32[2,64,512]{2,1,0:T(8,128)S(1)}, f32[2,64,512]{2,1,0:T(8,128)}, u32[]{:S(2)}) copy-start(f32[2,64,512]{2,1,0:T(8,128)} %param.13) | copy-start | bytes 786436
  95.0 384.7 %all-reduce.3.cloned.1.call-start = ((), (), s32[]{:S(2)}) async-start(), calls=%async_computation.6 | async-start | bytes 6291456 | tf_op jit(solution)/shard_map/psum | solution.py:50
  146.8 349.3 %copy-start.15 = (f32[4,128,128]{1,2,0:T(8,128)}, f32[4,128,128]{1,2,0:T(8,128)S(1)}, u32[]{:S(2)}) copy-start(f32[4,128,128]{1,2,0:T(8,128)S(1)} %custom-call.17) | copy-start | bytes 786436
  154.8 0.7 copy-start.21
  195.7 14.9 %copy-start.6 = (f32[4,128,128]{1,2,0:T(8,128)}, f32[4,128,128]{1,2,0:T(8,128)S(1)}, u32[]{:S(2)}) copy-start(f32[4,128,128]{1,2,0:T(8,128)S(1)} %custom-call.21) | copy-start | bytes 786436
  488.2 1.2 copy-start.5
  498.1 4.9 copy-start.9
  498.3 1.4 copy-start.11
  498.4 1.3 copy-start.12
  499.7 0.7 copy-start.13
  503.0 3.8 copy-start.7
  508.6 1.4 copy-start.14
  510.1 0.7 copy-start.16
  515.2 2.6 copy-start.18
  517.8 3.4 copy-start.2
  523.1 4.9 copy-start.8
  527.9 1.2 copy-start.4
  540.5 0.7 copy-start.17
  541.2 2.5 copy-start.10
Sparse Core Ops, SparseCore 0:
  51.4 60.9 reduce-scatter.2
  114.8 59.0 reduce-scatter.4
  210.7 268.9 all-reduce.2
